TPU v7x, 32 devices: a whole 2x2x4 slice. The times are simulated.
32 devices in a mesh: rows: 4 (over y, x), cols: 8 (over z, core).
Axes of the slice: x: 2, y: 2, z: 4, core: 2. Of those that a mesh axis runs over, the one named last changes fastest.
Arguments:
- anomalies: float32 [16384, 1024], P('rows', 'cols'), may hold values from -75 to 75
- pairing: int32 [2, 8], replicated, may hold values from 0 to 7, as said below
Outputs:
- rotated: float32 [16384, 1024], P('rows', 'cols')
Inputs may be any that keep to these rules, and one draw needn't show every extreme that they name: pairing[r, b] = b XOR m_r with one m_r for the whole row r; m_0 is neither 0 nor 1024 // 128 - 1, and for odd r m_r is m_0 with every bit of 7 flipped, for even r it is m_0.
All inputs are finite; a program needn't handle non-finite values.
Results may differ from a plain program's by a relative error of at most 0.0003.
Values sent between devices are 32-bit elements; how exact they have to be, the bound alone decides.
A program may use at most 128 MiB of HBM per device.

v0:
```python
from functools import partial

import jax
import jax.numpy as jnp
from jax import lax
from jax.experimental import pallas as pl
from jax.experimental.pallas import tpu as pltpu
from jax.sharding import PartitionSpec as P

SHIFTS = 8
TIE_GUARD = 1e-06
BAND = 2 * SHIFTS
PAIRS = 10
MESH = pl.DeviceIdType.MESH
HIGHEST = lax.Precision.HIGHEST


def dot(left, right):
    return jnp.dot(left, right, precision=HIGHEST, preferred_element_type=jnp.float32)


def dot_t(left, right):
    return lax.dot_general(
        left,
        right,
        (((0,), (0,)), ((), ())),
        precision=HIGHEST,
        preferred_element_type=jnp.float32,
    )


def exchange_kernel(count, make_piece, out_ref, send_sem, recv_sem, local_sem):
    me = lax.axis_index("cols")
    chips = count // 2
    chip = me // 2
    core = me % 2
    side = 1 - 2 * (chip // (chips // 2))

    barrier = pltpu.get_barrier_semaphore()
    for d in range(1, count):
        pl.semaphore_signal(
            barrier, inc=1, device_id={"cols": (me + d) % count}, device_id_type=MESH
        )
    copies = []
    for k in [*range(1, chips), 0]:
        for flip in (0, 1):
            if k == 0 and flip == 0:
                continue
            dest_chip = (chip + side * k + chips) % chips
            dest = dest_chip * 2 + (core + flip) % 2
            piece = make_piece(len(copies), dest)
            if not copies:
                pl.semaphore_wait(barrier, count - 1)
            copy = pltpu.make_async_remote_copy(
                src_ref=piece,
                dst_ref=out_ref.at[me],
                send_sem=send_sem.at[len(copies)],
                recv_sem=recv_sem.at[me],
                device_id={"cols": dest},
                device_id_type=MESH,
            )
            copy.start()
            copies.append(copy)
    local = pltpu.make_async_copy(make_piece(count - 1, me), out_ref.at[me], local_sem)
    local.start()
    local.wait()
    for d in range(1, count):
        source = (me + d) % count
        pltpu.make_async_remote_copy(
            src_ref=copies[0].src_ref,
            dst_ref=out_ref.at[source],
            send_sem=send_sem.at[0],
            recv_sem=recv_sem.at[source],
            device_id={"cols": source},
            device_id_type=MESH,
        ).wait_recv()
    for copy in copies:
        copy.wait_send()


def gather_kernel(count, x_ref, out_ref, *sems):
    exchange_kernel(count, lambda i, dest: x_ref.at[dest], out_ref, *sems)


def halves(value):
    high = value.astype(jnp.bfloat16)
    return high, (value - high.astype(jnp.float32)).astype(jnp.bfloat16)


def dot_3(left, right):
    a, b = halves(left)
    c, d = halves(right)
    product = partial(jnp.dot, preferred_element_type=jnp.float32)
    return product(a, c) + (product(a, d) + product(b, c))


def return_kernel(count, pairing, x_ref, coef_ref, out_ref, piece_ref, *sems):
    masks = (pairing[0, 0], pairing[1, 0], count - 1)

    def make_piece(i, dest):
        blocks = [x_ref[dest]] + [x_ref[dest ^ mask] for mask in masks]
        piece_ref[i] = dot_3(jnp.concatenate(blocks, axis=1), coef_ref[dest])
        return piece_ref.at[i]

    exchange_kernel(count, make_piece, out_ref, *sems)


def exchange_sems(count):
    return [
        pltpu.SemaphoreType.DMA((count - 1,)),
        pltpu.SemaphoreType.DMA((count,)),
        pltpu.SemaphoreType.DMA,
    ]


def turn_and_return(pairing, x, coef):
    count = x.shape[0]
    return pl.pallas_call(
        partial(return_kernel, count),
        out_shape=jax.ShapeDtypeStruct(x.shape, x.dtype),
        in_specs=[
            pl.BlockSpec(memory_space=pltpu.SMEM),
            pl.BlockSpec(memory_space=pltpu.VMEM),
            pl.BlockSpec(memory_space=pltpu.VMEM),
        ],
        out_specs=pl.BlockSpec(memory_space=pl.ANY),
        scratch_shapes=[pltpu.VMEM(x.shape, x.dtype), *exchange_sems(count)],
        compiler_params=pltpu.CompilerParams(collective_id=2, has_side_effects=True),
    )(pairing, x, coef)


def exchange(x, collective_id):
    count = x.shape[0]
    return pl.pallas_call(
        partial(gather_kernel, count),
        out_shape=jax.ShapeDtypeStruct(x.shape, x.dtype),
        in_specs=[pl.BlockSpec(memory_space=pl.ANY)],
        out_specs=pl.BlockSpec(memory_space=pl.ANY),
        scratch_shapes=exchange_sems(count),
        compiler_params=pltpu.CompilerParams(
            collective_id=collective_id, has_side_effects=True
        ),
    )(x)


def quad_blocks(pairing, count, g):
    m0 = pairing[0, 0]
    m1 = pairing[1, 0]
    lower_mask = jnp.minimum(m0, m1)
    low_bits = jnp.int32(0)
    for bit in range(1, count.bit_length() - 1):
        low_bits = jnp.where(lower_mask >= (1 << bit), (1 << bit) - 1, low_bits)
    rest = g & low_bits
    q0 = rest + 2 * (g - rest)
    return q0, q0 ^ m0, q0 ^ m1, q0 ^ (count - 1)


def lane_bit(shape, bit):
    return (lax.broadcasted_iota(jnp.int32, shape, 1) & (1 << bit)) != 0


def to_bands(block):
    w = block.shape[0]
    for bit in range(w.bit_length() - 1):
        block = jnp.where(
            lane_bit(block.shape, bit), pltpu.roll(block, w - (1 << bit), 0), block
        )
    return jnp.concatenate([block[w - BAND :], block[:BAND]], axis=0)


def from_bands(bands):
    w = bands.shape[1]
    block = jnp.concatenate(
        [bands[BAND:], jnp.zeros((w - 2 * BAND, w), jnp.float32), bands[:BAND]], axis=0
    )
    for bit in range(w.bit_length() - 1):
        block = jnp.where(lane_bit(block.shape, bit), pltpu.roll(block, 1 << bit, 0), block)
    return block


def gram_kernel(pairing, x_0, x_1, x_2, x_3, band_ref):
    g = pl.program_id(0)
    w = x_0.shape[2]
    lo, hi = slice(0, w), slice(w, 2 * w)
    a = jnp.concatenate([x_0[0], x_1[0]], axis=1)
    b = jnp.concatenate([x_2[0], x_3[0]], axis=1)
    aa, bb, ba = dot_t(a, a), dot_t(b, b), dot_t(b, a)
    blocks = [aa[lo, lo], aa[hi, lo], aa[hi, hi], bb[lo, lo], bb[hi, lo], bb[hi, hi]]
    blocks += [ba[lo, lo], ba[lo, hi], ba[hi, lo], ba[hi, hi]]

    @pl.when(g == 0)
    def _():
        band_ref[...] = jnp.zeros_like(band_ref)

    for i, block in enumerate(blocks):
        start = pl.multiple_of((g * PAIRS + i) * 2 * BAND, 2 * BAND)
        band_ref[pl.ds(start, 2 * BAND), :] = to_bands(block)


def gram(pairing, x, total):
    count = x.shape[0]

    def member(i):
        return pl.BlockSpec(
            (1, *x.shape[1:]), lambda g, pairing: (quad_blocks(pairing, count, g)[i], 0, 0)
        )

    return pl.pallas_call(
        gram_kernel,
        grid_spec=pltpu.PrefetchScalarGridSpec(
            num_scalar_prefetch=1,
            grid=(count // 4,),
            in_specs=[member(i) for i in range(4)],
            out_specs=pl.BlockSpec(memory_space=pltpu.VMEM),
        ),
        out_shape=jax.ShapeDtypeStruct((total, x.shape[2]), jnp.float32),
    )(pairing, x, x, x, x)


def sum_kernel(x_ref, out_ref, landed, part, slots, whole, send_sem, recv_sem):
    rows, cols = x_ref.shape[0], x_ref.shape[1]
    r, c = lax.axis_index("rows"), lax.axis_index("cols")
    barrier = pltpu.get_barrier_semaphore()
    for d in range(1, rows):
        pl.semaphore_signal(barrier, inc=1, device_id={"rows": (r + d) % rows}, device_id_type=MESH)
    for d in range(1, cols):
        pl.semaphore_signal(barrier, inc=1, device_id={"cols": (c + d) % cols}, device_id_type=MESH)
    pl.semaphore_wait(barrier, rows + cols - 2)

    def stage(number, axis, me, count, source, dest):
        copies = []
        for d in range(1, count):
            peer = (me + d) % count
            copy = pltpu.make_async_remote_copy(
                src_ref=source(peer),
                dst_ref=dest(d),
                send_sem=send_sem.at[number, d],
                recv_sem=recv_sem.at[number, d],
                device_id={axis: peer},
                device_id_type=MESH,
            )
            copy.start()
            copies.append(copy)
        for copy in copies:
            copy.wait_recv()
        return copies

    def finish(copies):
        for copy in copies:
            copy.wait_send()

    sent = stage(0, "rows", r, rows, lambda p: x_ref.at[p], lambda d: landed.at[d])
    total = x_ref[r]
    for d in range(1, rows):
        total = total + landed[d]
    part[...] = total
    sent += stage(1, "cols", c, cols, lambda p: part.at[p], lambda d: slots.at[d])
    total = part[c]
    for d in range(1, cols):
        total = total + slots[d]
    whole[c] = total
    sent += stage(2, "cols", c, cols, lambda p: whole.at[c], lambda d: whole.at[c])
    out_ref[r] = whole[...]
    sent += stage(3, "rows", r, rows, lambda p: whole, lambda d: out_ref.at[r])
    finish(sent)


def sum_all(x, rows, cols):
    total, width = x.shape
    piece = total // (rows * cols)
    peers = max(rows, cols)
    summed = pl.pallas_call(
        sum_kernel,
        out_shape=jax.ShapeDtypeStruct((rows, cols, piece, width), jnp.float32),
        in_specs=[pl.BlockSpec(memory_space=pltpu.VMEM)],
        out_specs=pl.BlockSpec(memory_space=pltpu.VMEM),
        scratch_shapes=[
            pltpu.VMEM((rows, cols, piece, width), jnp.float32),
            pltpu.VMEM((cols, piece, width), jnp.float32),
            pltpu.VMEM((cols, piece, width), jnp.float32),
            pltpu.VMEM((cols, piece, width), jnp.float32),
            pltpu.SemaphoreType.DMA((4, peers)),
            pltpu.SemaphoreType.DMA((4, peers)),
        ],
        compiler_params=pltpu.CompilerParams(collective_id=3, has_side_effects=True),
    )(x.reshape(rows, cols, piece, width))
    return summed.reshape(total, width)


def turn_pairs(gram, turn, pairs):
    _, depth, sides, w = gram.shape

    def lane(value):
        return pltpu.roll(value.reshape(depth * sides, w), w - 1, 1).reshape(depth, sides, w)

    def later(value):
        return jnp.concatenate([value[-1:], value[:-1]], axis=0)

    def sooner(value):
        return jnp.concatenate([value[1:], value[:1]], axis=0)

    def swap(value):
        return jnp.concatenate([value[:, pairs:], value[:, :pairs]], axis=1)

    def ahead(value):
        return jnp.stack([pltpu.roll(value, (BAND - r) % w, 1) if r != BAND else value for r in range(depth)])

    lower = lax.broadcasted_iota(jnp.int32, (depth, sides, w), 1) >= pairs

    @pl.loop(0, SHIFTS)
    def _(step):
        g_l, g_r = gram[0], gram[1]
        a, e, g = gram[0, BAND, :pairs], gram[1, BAND, pairs:], gram[1, BAND, :pairs]
        gap = e - a
        sign = jnp.where(gap >= 0.0, 1.0, -1.0)
        denom = jnp.abs(gap) + jnp.sqrt(gap * gap + 4.0 * g * g) + TIE_GUARD * (a + e)
        tangent = 2.0 * g * sign / denom
        cosine = 1.0 / jnp.sqrt(1.0 + tangent * tangent)
        sine = cosine * tangent
        c_2 = jnp.concatenate([cosine, cosine], axis=0)
        s_2 = jnp.concatenate([sine, sine], axis=0)
        c_d = ahead(c_2)
        s_d = ahead(jnp.concatenate([-sine, sine], axis=0))
        t_l = g_l * c_2 - g_r * s_2
        t_r = g_l * s_2 + g_r * c_2
        t_l = c_d * t_l + s_d * swap(t_l)
        t_r = lane(c_d * t_r + s_d * swap(t_r))
        gram[0] = jnp.where(lower, sooner(t_l), t_l)
        gram[1] = jnp.where(lower, t_r, later(t_r))
        v_l, v_r = turn[0], turn[1]
        turn[0] = v_l * c_2 - v_r * s_2
        turn[1] = later(lane(v_l * s_2 + v_r * c_2))


def rotate_kernel(groups, pairing, band_ref, coef_ref, turn_ref, gram, turn):
    w = band_ref.shape[1]
    pairs = 2 * groups
    lo, hi = slice(0, w), slice(w, 2 * w)

    def bands(g, i):
        start = (g * PAIRS + i) * 2 * BAND
        return band_ref[start : start + 2 * BAND, :]

    def reset_turns():
        shape = turn.shape
        one = lax.broadcasted_iota(jnp.int32, shape, 1) == BAND
        lower = lax.broadcasted_iota(jnp.int32, shape, 2) >= pairs
        right = lax.broadcasted_iota(jnp.int32, shape, 0) == 1
        turn[...] = jnp.where(one & (lower == right), 1.0, 0.0)

    def put_turns(slot):
        for g in range(groups):
            for p in range(2):
                at = 2 * g + p
                for row, side in ((lo, at), (hi, pairs + at)):
                    turn_ref[g, slot + p, row, lo] = from_bands(turn[0, :, side, :])
                    moved = from_bands(turn[1, :, side, :])
                    turn_ref[g, slot + p, row, hi] = pltpu.roll(moved, SHIFTS, 1)

    def put_gram(at, ll, lr, rl, rr):
        gram[0, :, at, :] = ll
        gram[1, :, at, :] = lr
        gram[0, :, pairs + at, :] = rl
        gram[1, :, pairs + at, :] = rr

    for g in range(groups):
        for p in range(2):
            below = bands(g, 3 * p + 1)
            above = to_bands(from_bands(below).T)
            put_gram(2 * g + p, bands(g, 3 * p), above, below, bands(g, 3 * p + 2))
    reset_turns()
    turn_pairs(gram, turn, pairs)
    put_turns(0)

    for g in range(groups):
        blocks = [from_bands(bands(g, 6 + i)) for i in range(4)]
        cross = jnp.concatenate(
            [
                jnp.concatenate([blocks[0], blocks[1]], axis=1),
                jnp.concatenate([blocks[2], blocks[3]], axis=1),
            ],
            axis=0,
        )
        half = dot(cross, turn_ref[g, 0])
        below = [
            dot_t(turn_ref[g, 1, :, lo], half[:, lo]),
            dot_t(turn_ref[g, 1, :, hi], half[:, hi]),
        ]
        a, b = 2 * g, 2 * g + 1
        a_lo, b_lo = gram[0, :, a, :], gram[0, :, b, :]
        a_hi = pltpu.roll(gram[1, :, pairs + a, :], SHIFTS, 1)
        b_hi = pltpu.roll(gram[1, :, pairs + b, :], SHIFTS, 1)
        put_gram(a, a_lo, to_bands(below[0].T), to_bands(below[0]), b_lo)
        put_gram(b, a_hi, to_bands(below[1].T), to_bands(below[1]), b_hi)
    reset_turns()
    turn_pairs(gram, turn, pairs)
    put_turns(2)

    for g in range(groups):
        q = quad_blocks(pairing, 4 * groups, g)
        for side, part in ((0, lo), (1, hi)):
            last = turn_ref.at[g, 2 + side]
            top = dot(turn_ref[g, 0, :, part], last[lo, :])
            bottom = dot(turn_ref[g, 1, :, part], last[hi, :])
            rows = [top[lo], top[hi], bottom[lo], bottom[hi]]
            for member, cols in ((side, lo), (2 + side, hi)):
                for i in range(4):
                    coef_ref[q[member], i * w : (i + 1) * w, :] = rows[member ^ i][:, cols]


def rotate(pairing, bands, groups):
    w = bands.shape[1]
    state = pltpu.VMEM((2, 2 * BAND, 4 * groups, w), jnp.float32)
    return pl.pallas_call(
        partial(rotate_kernel, groups),
        in_specs=[
            pl.BlockSpec(memory_space=pltpu.SMEM),
            pl.BlockSpec(memory_space=pltpu.VMEM),
        ],
        out_specs=pl.BlockSpec(memory_space=pltpu.VMEM),
        out_shape=jax.ShapeDtypeStruct((4 * groups, 4 * w, w), jnp.float32),
        scratch_shapes=[
            pltpu.VMEM((groups, 4, 2 * w, 2 * w), jnp.float32),
            state,
            state,
        ],
    )(pairing, bands)


def on_device(anomalies, pairing):
    count = lax.axis_size("cols")
    rows, width = anomalies.shape
    x = exchange(anomalies.reshape(count, rows // count, width), 1)
    split = lax.axis_size("rows")
    groups = count // 4
    unit = 8 * split * count
    total = -(-groups * PAIRS * 2 * BAND // unit) * unit
    bands = sum_all(gram(pairing, x, total), split, count)
    coef = rotate(pairing, bands, groups)
    return turn_and_return(pairing, x, coef).reshape(rows, width)


def solution(mesh):
    placed = (P("rows", "cols"), P())
    return jax.shard_map(
        on_device, mesh=mesh, in_specs=placed, out_specs=P("rows", "cols"), check_vma=False
    )
```

profile of v0, /device:TPU:0, one launch (start us, length us, event | category | flops | bytes accessed | tf_op | source)
XLA Modules:
  0.0 149.2 jit_solution(1811254010712987690)
XLA Ops:
  0.0 51.4 %shard_map.28.x_0.x_1.x_2.x_3.x_ref = f32[8,512,128]{2,1,0:T(8,128)} custom-call(f32[8,512,128]{2,1,0:T(8,128)} %bitcast.5), custom_call_target="tpu_custom_call" | custom-call | tf_op jit(solution)/shard_map/pallas_call | solution.py:134
  51.5 6.3 %shard_map.29 = f32[768,128]{1,0:T(8,128)} custom-call(s32[2,8]{1,0:T(2,128)} %pairing.5, f32[8,512,128]{2,1,0:T(8,128)} %shard_map.28.x_0.x_1.x_2.x_3.x_ref, f32[8,512,128]{2,1,0:T(8,128)} %shard_map.28.x_0.x_1.x_2.x_3.x_ref, f32[8,512,128]{2,1,0:T(8,128)} %shard_map.28.x_0.x_1.x_2.x_3.x_ref, f32[8,512,128]{2,1,0:T(8,128)} %shard_map.28.x_0.x_1.x_2.x_3.x_ref), custom_call_target="tpu_custom_call" | custom-call | tf_op jit(solution)/shard_map/pallas_call | solution.py:208
  57.8 26.0 %shard_map.30 = f32[4,8,24,128]{3,2,1,0:T(8,128)} custom-call(f32[4,8,24,128]{3,2,1,0:T(8,128)} %bitcast.6), custom_call_target="tpu_custom_call" | custom-call | tf_op jit(solution)/shard_map/pallas_call | solution.py:272
  83.8 11.5 %shard_map.31.coef_ref = f32[8,512,128]{2,1,0:T(8,128)} custom-call(s32[2,8]{1,0:T(2,128)} %pairing.5, f32[768,128]{1,0:T(8,128)} %bitcast.7), custom_call_target="tpu_custom_call" | custom-call | tf_op jit(solution)/shard_map/pallas_call | solution.py:414
  95.3 50.8 %shard_map.32 = f32[8,512,128]{2,1,0:T(8,128)} custom-call(s32[2,8]{1,0:T(2,128)} %pairing.5, f32[8,512,128]{2,1,0:T(8,128)} %shard_map.28.x_0.x_1.x_2.x_3.x_ref, f32[8,512,128]{2,1,0:T(8,128)} %shard_map.31.coef_ref), custom_call_target="tpu_custom_call" | custom-call | tf_op jit(solution)/shard_map/pallas_call | solution.py:118
  146.2 3.0 %copy.4 = f32[4096,128]{1,0:T(8,128)} copy(f32[4096,128]{1,0:T(8,128)} %bitcast.4) | data formatting | bytes 4194304
where the time goes:
time: 149 us
  Pallas kernels  146 us (98%)
  local copies, waits for them, and re-layouts  3.05 us (2%)
    pallas_call x1, Pallas kernels, exchange(): pl.pallas_call(partial(gather_kernel, count), out_shape=jax.ShapeDtypeStr...  51.4 us
    pallas_call x1, Pallas kernels, turn_and_return(): pl.pallas_call(partial(return_kernel, count), out_shape=jax.ShapeDtypeStr...  50.8 us
    pallas_call x1, Pallas kernels, sum_all(): pl.pallas_call(sum_kernel, out_shape=jax.ShapeDtypeStruct((rows, cols, pi...  26 us
    pallas_call x1, Pallas kernels, rotate(): pl.pallas_call(partial(rotate_kernel, groups), in_specs=[pl.BlockSpec(mem...  11.5 us
    pallas_call x1, Pallas kernels, gram(): pl.pallas_call(gram_kernel, grid_spec=pltpu.PrefetchScalarGridSpec(num_sc...  6.34 us
    unnamed x1, local copies, waits for them, and re-layouts  3.05 us

commit v1 on v0

v1 whole, which is shorter than its diff:
```python
from functools import partial

import jax
import jax.numpy as jnp
from jax import lax
from jax.experimental import pallas as pl
from jax.experimental.pallas import tpu as pltpu
from jax.sharding import PartitionSpec as P

SHIFTS = 8
TIE_GUARD = 1e-06
BAND = 2 * SHIFTS
PAIRS = 10
MESH = pl.DeviceIdType.MESH
HIGHEST = lax.Precision.HIGHEST
UNITS = 8
PARTS = (3, 3, 1, 1)
EXTRAS = (2, 1, 3)


def dot(left, right):
    return jnp.dot(left, right, precision=HIGHEST, preferred_element_type=jnp.float32)


def dot_t(left, right):
    return lax.dot_general(
        left,
        right,
        (((0,), (0,)), ((), ())),
        precision=HIGHEST,
        preferred_element_type=jnp.float32,
    )


def halves(value):
    high = value.astype(jnp.bfloat16)
    return high, (value - high.astype(jnp.float32)).astype(jnp.bfloat16)


def dot_3(left, right):
    a, b = halves(left)
    c, d = halves(right)
    product = partial(jnp.dot, preferred_element_type=jnp.float32)
    return product(a, c) + (product(a, d) + product(b, c))


def quad_blocks(pairing, count, g):
    m0 = pairing[0, 0]
    m1 = pairing[1, 0]
    lower_mask = jnp.minimum(m0, m1)
    low_bits = jnp.int32(0)
    for bit in range(1, count.bit_length() - 1):
        low_bits = jnp.where(lower_mask >= (1 << bit), (1 << bit) - 1, low_bits)
    rest = g & low_bits
    q0 = rest + 2 * (g - rest)
    return q0, q0 ^ m0, q0 ^ m1, q0 ^ (count - 1)


def lane_bit(shape, bit):
    return (lax.broadcasted_iota(jnp.int32, shape, 1) & (1 << bit)) != 0


def to_bands(block):
    w = block.shape[0]
    for bit in range(w.bit_length() - 1):
        block = jnp.where(
            lane_bit(block.shape, bit), pltpu.roll(block, w - (1 << bit), 0), block
        )
    return jnp.concatenate([block[w - BAND :], block[:BAND]], axis=0)


def from_bands(bands):
    w = bands.shape[1]
    block = jnp.concatenate(
        [bands[BAND:], jnp.zeros((w - 2 * BAND, w), jnp.float32), bands[:BAND]], axis=0
    )
    for bit in range(w.bit_length() - 1):
        block = jnp.where(lane_bit(block.shape, bit), pltpu.roll(block, 1 << bit, 0), block)
    return block


def turn_pairs(gram, turn, pairs):
    _, depth, sides, w = gram.shape

    def lane(value):
        return pltpu.roll(value.reshape(depth * sides, w), w - 1, 1).reshape(depth, sides, w)

    def later(value):
        return jnp.concatenate([value[-1:], value[:-1]], axis=0)

    def sooner(value):
        return jnp.concatenate([value[1:], value[:1]], axis=0)

    def swap(value):
        return jnp.concatenate([value[:, pairs:], value[:, :pairs]], axis=1)

    def ahead(value):
        return jnp.stack([pltpu.roll(value, (BAND - r) % w, 1) if r != BAND else value for r in range(depth)])

    lower = lax.broadcasted_iota(jnp.int32, (depth, sides, w), 1) >= pairs

    @pl.loop(0, SHIFTS)
    def _(step):
        g_l, g_r = gram[0], gram[1]
        a, e, g = gram[0, BAND, :pairs], gram[1, BAND, pairs:], gram[1, BAND, :pairs]
        gap = e - a
        sign = jnp.where(gap >= 0.0, 1.0, -1.0)
        denom = jnp.abs(gap) + jnp.sqrt(gap * gap + 4.0 * g * g) + TIE_GUARD * (a + e)
        tangent = 2.0 * g * sign / denom
        cosine = 1.0 / jnp.sqrt(1.0 + tangent * tangent)
        sine = cosine * tangent
        c_2 = jnp.concatenate([cosine, cosine], axis=0)
        s_2 = jnp.concatenate([sine, sine], axis=0)
        c_d = ahead(c_2)
        s_d = ahead(jnp.concatenate([-sine, sine], axis=0))
        t_l = g_l * c_2 - g_r * s_2
        t_r = g_l * s_2 + g_r * c_2
        t_l = c_d * t_l + s_d * swap(t_l)
        t_r = lane(c_d * t_r + s_d * swap(t_r))
        gram[0] = jnp.where(lower, sooner(t_l), t_l)
        gram[1] = jnp.where(lower, t_r, later(t_r))
        v_l, v_r = turn[0], turn[1]
        turn[0] = v_l * c_2 - v_r * s_2
        turn[1] = later(lane(v_l * s_2 + v_r * c_2))


def spans(sizes, unit):
    out, at = [], 0
    for size in sizes:
        out.append((at * unit, (at + size) * unit))
        at += size
    return out


def fused_kernel(count, split, unit, names, pairing, x_ref, out_ref, *refs):
    ref = dict(zip(names, refs))
    near = [ref["near%d" % i] for i in range(len(PARTS))]
    far = [ref["far%d" % i] for i in range(len(EXTRAS))]
    near_at, far_at = spans(PARTS, unit), spans(EXTRAS, unit)
    slab, kept = UNITS * unit, sum(EXTRAS) * unit
    half, groups = count // 2, count // 4
    w = x_ref.shape[2]
    lo, hi = slice(0, w), slice(w, 2 * w)
    me, r = lax.axis_index("cols"), lax.axis_index("rows")
    side, pos = me // half, me % half
    across = [(1 - side) * half + (pos + j) % half for j in range(half)]
    beside = [side * half + (pos + j) % half for j in range(1, half)]
    others = across + beside
    masks = (pairing[0, 0], pairing[1, 0], count - 1)
    sent = []

    barrier = pltpu.get_barrier_semaphore()
    for dest in others:
        pl.semaphore_signal(barrier, inc=1, device_id={"cols": dest}, device_id_type=MESH)
    for d in range(1, split):
        pl.semaphore_signal(
            barrier, inc=1, device_id={"rows": (r + d) % split}, device_id_type=MESH
        )
    pl.semaphore_wait(barrier, count + split - 2)

    def remote(src, dst, send, recv, axis, peer):
        return pltpu.make_async_remote_copy(
            src_ref=src,
            dst_ref=dst,
            send_sem=send,
            recv_sem=recv,
            device_id={axis: peer},
            device_id_type=MESH,
        )

    def send(*args):
        copy = remote(*args)
        copy.start()
        sent.append(copy)

    def give(number, land, at, owner):
        rows = pl.ds(at[0], at[1] - at[0])
        for i, dest in enumerate(others):
            src = x_ref.at[owner(dest), rows]
            send(src, land.at[me], ref["give"].at[number, i], ref["get"].at[number, me], "cols", dest)

    def keep(number, land, at, owner):
        rows = pl.ds(at[0], at[1] - at[0])
        return pltpu.make_async_copy(x_ref.at[owner, rows], land.at[me], ref["own"].at[number])

    def take(number, land):
        for source in others:
            remote(
                land.at[source], land.at[source], ref["give"].at[number, 0], ref["get"].at[number, source], "cols", source
            ).wait_recv()

    def mirror(d):
        return count - 1 - d

    kept_copies = []
    for i, at in enumerate(near_at):
        give(i, near[i], at, lambda d: d)
        kept_copies.append(keep(i, near[i], at, me))
        kept_copies[-1].start()

    def give_far(i):
        n = len(PARTS) + i
        give(n, far[i], far_at[i], mirror)
        copy = keep(n, far[i], far_at[i], mirror(me))
        copy.start()
        kept_copies.append(copy)

    give_far(0)

    acc, bands = ref["acc"], ref["bands"]
    for i, land in enumerate(near):
        kept_copies[i].wait()
        take(i, land)
        for g in range(groups):
            x = [land[q] for q in quad_blocks(pairing, count, g)]
            a = jnp.concatenate(x[:2], axis=1)
            b = jnp.concatenate(x[2:], axis=1)
            for k, block in enumerate((dot_t(a, a), dot_t(b, b), dot_t(b, a))):
                acc[g, k] = block if i == 0 else acc[g, k] + block
    for g in range(groups):
        places = [(0, lo, lo), (0, hi, lo), (0, hi, hi), (1, lo, lo), (1, hi, lo), (1, hi, hi)]
        places += [(2, lo, lo), (2, lo, hi), (2, hi, lo), (2, hi, hi)]
        for i, (k, rows, cols) in enumerate(places):
            at = g * PAIRS + i
            bands[at // bands.shape[1], at % bands.shape[1]] = to_bands(acc[g, k, rows, cols])

    landed, part, slots, whole, summed = (
        ref[n] for n in ("landed", "part", "slots", "whole", "summed")
    )

    def stage(number, axis, me, n, source, dest):
        copies = []
        for d in range(1, n):
            peer = (me + d) % n
            copy = remote(
                source(peer), dest(d), ref["sum_s"].at[number, d], ref["sum_r"].at[number, d], axis, peer
            )
            copy.start()
            copies.append(copy)
        sent.extend(copies)
        return copies

    def arrive(copies):
        for copy in copies:
            copy.wait_recv()

    arrive(stage(0, "rows", r, split, lambda p: bands.at[p], lambda d: landed.at[d]))
    total = bands[r]
    for d in range(1, split):
        total = total + landed[d]
    part[...] = total.reshape(part.shape)
    copies = stage(1, "cols", me, count, lambda p: part.at[p], lambda d: slots.at[d])
    give_far(1)
    arrive(copies)
    total = part[me]
    for d in range(1, count):
        total = total + slots[d]
    whole[me] = total
    copies = stage(2, "cols", me, count, lambda p: whole.at[me], lambda d: whole.at[me])
    give_far(2)
    arrive(copies)
    summed[r] = whole[...]
    arrive(stage(3, "rows", r, split, lambda p: whole, lambda d: summed.at[r]))

    rotate(groups, summed[...].reshape(-1, w), ref["coef"], ref["turn_of"], ref["gram"], ref["turn"])

    segments = []
    for i, (start, stop) in enumerate(near_at):
        segments.append((near[i], start, stop, False))
    for i, (start, stop) in enumerate(far_at):
        segments.append((far[i], start, stop, True))

    def slot(dest):
        found = jnp.int32(0)
        for g in range(groups):
            for i, q in enumerate(quad_blocks(pairing, count, g)):
                found = jnp.where(q == dest, 4 * g + i, found)
        return found

    def place(owner, start, stop):
        return out_ref.at[owner, pl.ds(start, stop - start)]

    def make(dest, number, coef, buffer, first, rows):
        blocks = [buffer[dest, first : first + rows]]
        blocks += [buffer[dest ^ mask, first : first + rows] for mask in masks]
        high, low = halves(jnp.concatenate(blocks, axis=1))
        product = partial(jnp.dot, preferred_element_type=jnp.float32)
        return product(high, coef[0]) + (product(high, coef[1]) + product(low, coef[0]))

    beside_jobs, across_jobs = [], []
    for i, (buffer, start, stop, far_rows) in enumerate(segments):
        beside_jobs.append((i, buffer, 0, start, stop, far_rows))
        if not far_rows and stop > kept:
            first = max(start, kept)
            across_jobs.append((i, buffer, first - start, first, stop, far_rows))

    def emit(index, dest, job, coef):
        i, buffer, first, start, stop, far_rows = job
        piece_ref = ref["piece"].at[index, pl.ds(start + (slab if far_rows else 0), stop - start)]
        piece_ref[...] = make(dest, index, coef, buffer, first, stop - start)
        return piece_ref, place(mirror(me) if far_rows else me, start, stop)

    for i in range(len(EXTRAS)):
        take(len(PARTS) + i, far[i])
    for copy in kept_copies[len(PARTS) :]:
        copy.wait()

    for index, dest in enumerate(others):
        coef = halves(ref["coef"][slot(dest)])
        for job in across_jobs if index < half else beside_jobs:
            src, dst = emit(index, dest, job, coef)
            send(src, dst, ref["back_s"].at[index, job[0]], ref["back_r"].at[me, job[0]], "cols", dest)
    coef = halves(ref["coef"][slot(me)])
    local = []
    for job in beside_jobs:
        src, dst = emit(len(others), me, job, coef)
        local.append(pltpu.make_async_copy(src, dst, ref["home"].at[job[0]]))
        local[-1].start()
    for index, source in enumerate(others):
        for i, _, _, start, stop, far_rows in across_jobs if index < half else beside_jobs:
            dst = place(mirror(source) if far_rows else source, start, stop)
            remote(
                dst, dst, ref["back_s"].at[index, i], ref["back_r"].at[source, i], "cols", source
            ).wait_recv()
    for copy in local:
        copy.wait()
    for copy in sent:
        copy.wait_send()


def rotate(groups, band_ref, coef_ref, turn_ref, gram, turn):
    w = band_ref.shape[1]
    pairs = 2 * groups
    lo, hi = slice(0, w), slice(w, 2 * w)

    def bands(g, i):
        start = (g * PAIRS + i) * 2 * BAND
        return band_ref[start : start + 2 * BAND, :]

    def reset_turns():
        shape = turn.shape
        one = lax.broadcasted_iota(jnp.int32, shape, 1) == BAND
        lower = lax.broadcasted_iota(jnp.int32, shape, 2) >= pairs
        right = lax.broadcasted_iota(jnp.int32, shape, 0) == 1
        turn[...] = jnp.where(one & (lower == right), 1.0, 0.0)

    def put_turns(slot):
        for g in range(groups):
            for p in range(2):
                at = 2 * g + p
                for row, side in ((lo, at), (hi, pairs + at)):
                    turn_ref[g, slot + p, row, lo] = from_bands(turn[0, :, side, :])
                    moved = from_bands(turn[1, :, side, :])
                    turn_ref[g, slot + p, row, hi] = pltpu.roll(moved, SHIFTS, 1)

    def put_gram(at, ll, lr, rl, rr):
        gram[0, :, at, :] = ll
        gram[1, :, at, :] = lr
        gram[0, :, pairs + at, :] = rl
        gram[1, :, pairs + at, :] = rr

    for g in range(groups):
        for p in range(2):
            below = bands(g, 3 * p + 1)
            above = to_bands(from_bands(below).T)
            put_gram(2 * g + p, bands(g, 3 * p), above, below, bands(g, 3 * p + 2))
    reset_turns()
    turn_pairs(gram, turn, pairs)
    put_turns(0)

    for g in range(groups):
        blocks = [from_bands(bands(g, 6 + i)) for i in range(4)]
        cross = jnp.concatenate(
            [
                jnp.concatenate([blocks[0], blocks[1]], axis=1),
                jnp.concatenate([blocks[2], blocks[3]], axis=1),
            ],
            axis=0,
        )
        half = dot(cross, turn_ref[g, 0])
        below = [
            dot_t(turn_ref[g, 1, :, lo], half[:, lo]),
            dot_t(turn_ref[g, 1, :, hi], half[:, hi]),
        ]
        a, b = 2 * g, 2 * g + 1
        a_lo, b_lo = gram[0, :, a, :], gram[0, :, b, :]
        a_hi = pltpu.roll(gram[1, :, pairs + a, :], SHIFTS, 1)
        b_hi = pltpu.roll(gram[1, :, pairs + b, :], SHIFTS, 1)
        put_gram(a, a_lo, to_bands(below[0].T), to_bands(below[0]), b_lo)
        put_gram(b, a_hi, to_bands(below[1].T), to_bands(below[1]), b_hi)
    reset_turns()
    turn_pairs(gram, turn, pairs)
    put_turns(2)

    for g in range(groups):
        for side, part in ((0, lo), (1, hi)):
            last = turn_ref.at[g, 2 + side]
            top = dot(turn_ref[g, 0, :, part], last[lo, :])
            bottom = dot(turn_ref[g, 1, :, part], last[hi, :])
            rows = [top[lo], top[hi], bottom[lo], bottom[hi]]
            for member, cols in ((side, lo), (2 + side, hi)):
                for i in range(4):
                    coef_ref[4 * g + member, i * w : (i + 1) * w, :] = rows[member ^ i][:, cols]


def on_device(anomalies, pairing):
    count, split = lax.axis_size("cols"), lax.axis_size("rows")
    rows, w = anomalies.shape
    slab = rows // count
    unit = slab // UNITS
    groups = count // 4
    f32 = jnp.float32
    block = 8 * split * count
    total = -(-groups * PAIRS * 2 * BAND // block) * block
    piece = total // (split * count)
    extra = sum(EXTRAS) * unit
    segments = len(PARTS) + len(EXTRAS)
    peers = max(count, split)
    dma = pltpu.SemaphoreType.DMA
    scratch = {
        "acc": pltpu.VMEM((groups, 3, 2 * w, 2 * w), f32),
        "bands": pltpu.VMEM((split, total // split // (2 * BAND), 2 * BAND, w), f32),
        "landed": pltpu.VMEM((split, total // split // (2 * BAND), 2 * BAND, w), f32),
        "part": pltpu.VMEM((count, piece, w), f32),
        "slots": pltpu.VMEM((count, piece, w), f32),
        "whole": pltpu.VMEM((count, piece, w), f32),
        "summed": pltpu.VMEM((split, count, piece, w), f32),
        "turn_of": pltpu.VMEM((groups, 4, 2 * w, 2 * w), f32),
        "gram": pltpu.VMEM((2, 2 * BAND, 4 * groups, w), f32),
        "turn": pltpu.VMEM((2, 2 * BAND, 4 * groups, w), f32),
        "coef": pltpu.VMEM((4 * groups, 4 * w, w), f32),
        "piece": pltpu.VMEM((count, slab + extra, w), f32),
        "give": dma((segments, count - 1)),
        "get": dma((segments, count)),
        "own": dma((segments,)),
        "sum_s": dma((4, peers)),
        "sum_r": dma((4, peers)),
        "back_s": dma((count, segments)),
        "back_r": dma((count, segments)),
        "home": dma((segments,)),
    }
    for i, size in enumerate(PARTS):
        scratch["near%d" % i] = pltpu.VMEM((count, size * unit, w), f32)
    for i, size in enumerate(EXTRAS):
        scratch["far%d" % i] = pltpu.VMEM((count, size * unit, w), f32)
    out = pl.pallas_call(
        partial(fused_kernel, count, split, unit, tuple(scratch)),
        out_shape=jax.ShapeDtypeStruct((count, slab, w), f32),
        in_specs=[
            pl.BlockSpec(memory_space=pltpu.SMEM),
            pl.BlockSpec(memory_space=pl.ANY),
        ],
        out_specs=pl.BlockSpec(memory_space=pl.ANY),
        scratch_shapes=list(scratch.values()),
        compiler_params=pltpu.CompilerParams(collective_id=1, has_side_effects=True),
    )(pairing, anomalies.reshape(count, slab, w))
    return out.reshape(rows, w)


def solution(mesh):
    placed = (P("rows", "cols"), P())
    return jax.shard_map(
        on_device, mesh=mesh, in_specs=placed, out_specs=P("rows", "cols"), check_vma=False
    )
```

time: 149 us -> 135 us (0.906); the launches traced: 149 us -> 133 us
  Pallas kernels: 146 us -> 130 us
    pallas_call x5 -> x1, Pallas kernels: 146 us -> 130 us  [on_device(): pl.pallas_call(partial(fused_kernel, count, split, unit, tuple(scratch)),...]
where the time goes in v1:
time: 135 us; the launch traced here: 133 us
  Pallas kernels  130 us (96%)
  local copies, waits for them, and re-layouts  3.05 us (2%)
    pallas_call x1, Pallas kernels, on_device(): pl.pallas_call(partial(fused_kernel, count, split, unit, tuple(scratch)),...  130 us
    unnamed x1, local copies, waits for them, and re-layouts  3.05 us

profile of v1, /device:TPU:0, one launch (start us, length us, event | category | flops | bytes accessed | tf_op | source)
XLA Modules:
  0.0 132.6 jit_solution(17454339393407823415)
XLA Ops:
  0.0 129.6 %shard_map.28 = f32[8,512,128]{2,1,0:T(8,128)} custom-call(s32[2,8]{1,0:T(2,128)} %pairing.1, f32[8,512,128]{2,1,0:T(8,128)} %bitcast.3), custom_call_target="tpu_custom_call" | custom-call | tf_op jit(solution)/shard_map/pallas_call | solution.py:446
  129.6 3.0 %copy.4 = f32[4096,128]{1,0:T(8,128)} copy(f32[4096,128]{1,0:T(8,128)} %bitcast.2) | data formatting | bytes 4194304

commit v2 on v1

--- a/solution.py
+++ b/solution.py
@@ -15,7 +15,7 @@
 HIGHEST = lax.Precision.HIGHEST
 UNITS = 8
 PARTS = (3, 3, 1, 1)
-EXTRAS = (2, 1, 3)
+EXTRAS = (3, 2, 3)
 
 
 def dot(left, right):
@@ -146,8 +146,14 @@
     across = [(1 - side) * half + (pos + j) % half for j in range(half)]
     beside = [side * half + (pos + j) % half for j in range(1, half)]
     others = across + beside
+    ends = [0, 1, count - 2, count - 1]
     masks = (pairing[0, 0], pairing[1, 0], count - 1)
-    sent = []
+
+    def at_end(d):
+        return (d < 2) | (d >= count - 2)
+
+    def mirror(d):
+        return count - 1 - d
 
     barrier = pltpu.get_barrier_semaphore()
     for dest in others:
@@ -168,48 +174,54 @@
             device_id_type=MESH,
         )
 
-    def send(*args):
+    sent = []
+
+    def send(*args, when=None):
         copy = remote(*args)
-        copy.start()
-        sent.append(copy)
-
-    def give(number, land, at, owner):
-        rows = pl.ds(at[0], at[1] - at[0])
-        for i, dest in enumerate(others):
-            src = x_ref.at[owner(dest), rows]
-            send(src, land.at[me], ref["give"].at[number, i], ref["get"].at[number, me], "cols", dest)
+        sent.append((copy, when))
+        if when is None:
+            copy.start()
+        else:
+            pl.when(when)(copy.start)
 
     def keep(number, land, at, owner):
         rows = pl.ds(at[0], at[1] - at[0])
         return pltpu.make_async_copy(x_ref.at[owner, rows], land.at[me], ref["own"].at[number])
 
+    def give_near(i):
+        rows = pl.ds(near_at[i][0], near_at[i][1] - near_at[i][0])
+        for n, dest in enumerate(others):
+            send(x_ref.at[dest, rows], near[i].at[me], ref["give"].at[i, n], ref["get"].at[i, me], "cols", dest)
+
+    def give_far(i, crossing):
+        rows = pl.ds(far_at[i][0], far_at[i][1] - far_at[i][0])
+        n = len(PARTS) + i
+        for k, dest in enumerate(ends):
+            cross = (dest // half) != side
+            when = cross if crossing else jnp.logical_not(cross) & (dest != me)
+            send(x_ref.at[mirror(dest), rows], far[i].at[me], ref["give_s"].at[i, k], ref["get"].at[n, me], "cols", dest, when=when)
+
     def take(number, land):
         for source in others:
             remote(
-                land.at[source], land.at[source], ref["give"].at[number, 0], ref["get"].at[number, source], "cols", source
+                land.at[source], land.at[source], ref["give"].at[0, 0], ref["get"].at[number, source], "cols", source
             ).wait_recv()
 
-    def mirror(d):
-        return count - 1 - d
-
-    kept_copies = []
-    for i, at in enumerate(near_at):
-        give(i, near[i], at, lambda d: d)
-        kept_copies.append(keep(i, near[i], at, me))
-        kept_copies[-1].start()
-
-    def give_far(i):
-        n = len(PARTS) + i
-        give(n, far[i], far_at[i], mirror)
-        copy = keep(n, far[i], far_at[i], mirror(me))
+    near_keep = [keep(i, near[i], at, me) for i, at in enumerate(near_at)]
+    far_keep = [keep(len(PARTS) + i, far[i], at, mirror(me)) for i, at in enumerate(far_at)]
+    for copy in near_keep:
         copy.start()
-        kept_copies.append(copy)
-
-    give_far(0)
+    for copy in far_keep:
+        pl.when(at_end(me))(copy.start)
+    for i in range(len(PARTS)):
+        give_near(i)
+    for i in range(len(EXTRAS)):
+        give_far(i, False)
+    give_far(0, True)
 
     acc, bands = ref["acc"], ref["bands"]
     for i, land in enumerate(near):
-        kept_copies[i].wait()
+        near_keep[i].wait()
         take(i, land)
         for g in range(groups):
             x = [land[q] for q in quad_blocks(pairing, count, g)]
@@ -217,58 +229,60 @@
             b = jnp.concatenate(x[2:], axis=1)
             for k, block in enumerate((dot_t(a, a), dot_t(b, b), dot_t(b, a))):
                 acc[g, k] = block if i == 0 else acc[g, k] + block
+    places = [(0, lo, lo), (0, hi, lo), (0, hi, hi), (1, lo, lo), (1, hi, lo), (1, hi, hi)]
+    places += [(2, lo, lo), (2, lo, hi), (2, hi, lo), (2, hi, hi)]
     for g in range(groups):
-        places = [(0, lo, lo), (0, hi, lo), (0, hi, hi), (1, lo, lo), (1, hi, lo), (1, hi, hi)]
-        places += [(2, lo, lo), (2, lo, hi), (2, hi, lo), (2, hi, hi)]
         for i, (k, rows, cols) in enumerate(places):
-            at = g * PAIRS + i
-            bands[at // bands.shape[1], at % bands.shape[1]] = to_bands(acc[g, k, rows, cols])
-
-    landed, part, slots, whole, summed = (
-        ref[n] for n in ("landed", "part", "slots", "whole", "summed")
-    )
-
-    def stage(number, axis, me, n, source, dest):
-        copies = []
-        for d in range(1, n):
-            peer = (me + d) % n
-            copy = remote(
-                source(peer), dest(d), ref["sum_s"].at[number, d], ref["sum_r"].at[number, d], axis, peer
-            )
-            copy.start()
-            copies.append(copy)
-        sent.extend(copies)
-        return copies
-
-    def arrive(copies):
-        for copy in copies:
-            copy.wait_recv()
-
-    arrive(stage(0, "rows", r, split, lambda p: bands.at[p], lambda d: landed.at[d]))
-    total = bands[r]
+            first, size = band_place(g, i)
+            bands[first : first + size] = to_bands(acc[g, k, rows, cols])[2 * BAND - size :]
+
+    landed, slots, part, summed = (ref[n] for n in ("landed", "slots", "part", "summed"))
+    piece = slots.shape[1]
+
+    def at(row, col):
+        return pl.ds(pl.multiple_of((row * count + col) * piece, piece), piece)
+
+    for k, c in enumerate(others + [me]):
+        for d in range(1, split):
+            peer = (r + d) % split
+            send(bands.at[at(peer, c)], landed.at[d, k], ref["rs_s"].at[d, k], ref["rs_r"].at[d, k], "rows", peer)
+    for k, c in enumerate(others + [me]):
+        total = bands[at(r, c)]
+        for d in range(1, split):
+            peer = (r + split - d) % split
+            remote(landed.at[d, k], landed.at[d, k], ref["rs_s"].at[d, k], ref["rs_r"].at[d, k], "rows", peer).wait_recv()
+            total = total + landed[d, k]
+        part[k] = total
+        if k < len(others):
+            send(part.at[k], slots.at[me], ref["sum_s"].at[0, k], ref["sum_r"].at[0, me], "cols", c)
+    give_far(1, True)
+    for c in others:
+        remote(slots.at[c], slots.at[c], ref["sum_s"].at[0, 0], ref["sum_r"].at[0, c], "cols", c).wait_recv()
+        total = total + slots[c]
+    summed[at(r, me)] = total
+    mine = summed.at[at(r, me)]
+
+    def spread(source, k):
+        for d in range(1, split):
+            peer = (r + d) % split
+            block = summed.at[at(r, source)]
+            send(block, block, ref["ag_s"].at[d, k], ref["ag_r"].at[r, k], "rows", peer)
+
+    for k, c in enumerate(others):
+        send(mine, mine, ref["sum_s"].at[1, k], ref["sum_r"].at[1, me], "cols", c)
+    spread(me, len(others))
+    give_far(2, True)
+    for k, c in reversed(list(enumerate(others))):
+        block = summed.at[at(r, c)]
+        remote(block, block, ref["sum_s"].at[1, k], ref["sum_r"].at[1, c], "cols", c).wait_recv()
+        spread(c, k)
     for d in range(1, split):
-        total = total + landed[d]
-    part[...] = total.reshape(part.shape)
-    copies = stage(1, "cols", me, count, lambda p: part.at[p], lambda d: slots.at[d])
-    give_far(1)
-    arrive(copies)
-    total = part[me]
-    for d in range(1, count):
-        total = total + slots[d]
-    whole[me] = total
-    copies = stage(2, "cols", me, count, lambda p: whole.at[me], lambda d: whole.at[me])
-    give_far(2)
-    arrive(copies)
-    summed[r] = whole[...]
-    arrive(stage(3, "rows", r, split, lambda p: whole, lambda d: summed.at[r]))
-
-    rotate(groups, summed[...].reshape(-1, w), ref["coef"], ref["turn_of"], ref["gram"], ref["turn"])
-
-    segments = []
-    for i, (start, stop) in enumerate(near_at):
-        segments.append((near[i], start, stop, False))
-    for i, (start, stop) in enumerate(far_at):
-        segments.append((far[i], start, stop, True))
+        row = (r + d) % split
+        for k, c in enumerate(others + [me]):
+            block = summed.at[at(row, c)]
+            remote(block, block, ref["ag_s"].at[d, k], ref["ag_r"].at[row, k], "rows", row).wait_recv()
+
+    rotate(groups, summed, ref["coef"], ref["turn_of"], ref["gram"], ref["turn"])
 
     def slot(dest):
         found = jnp.int32(0)
@@ -277,55 +291,84 @@
                 found = jnp.where(q == dest, 4 * g + i, found)
         return found
 
-    def place(owner, start, stop):
-        return out_ref.at[owner, pl.ds(start, stop - start)]
-
-    def make(dest, number, coef, buffer, first, rows):
-        blocks = [buffer[dest, first : first + rows]]
-        blocks += [buffer[dest ^ mask, first : first + rows] for mask in masks]
+    def make(dest, coef, buffer):
+        blocks = [buffer[dest]] + [buffer[dest ^ mask] for mask in masks]
         high, low = halves(jnp.concatenate(blocks, axis=1))
         product = partial(jnp.dot, preferred_element_type=jnp.float32)
         return product(high, coef[0]) + (product(high, coef[1]) + product(low, coef[0]))
 
-    beside_jobs, across_jobs = [], []
-    for i, (buffer, start, stop, far_rows) in enumerate(segments):
-        beside_jobs.append((i, buffer, 0, start, stop, far_rows))
-        if not far_rows and stop > kept:
-            first = max(start, kept)
-            across_jobs.append((i, buffer, first - start, first, stop, far_rows))
-
-    def emit(index, dest, job, coef):
-        i, buffer, first, start, stop, far_rows = job
-        piece_ref = ref["piece"].at[index, pl.ds(start + (slab if far_rows else 0), stop - start)]
-        piece_ref[...] = make(dest, index, coef, buffer, first, stop - start)
-        return piece_ref, place(mirror(me) if far_rows else me, start, stop)
-
-    for i in range(len(EXTRAS)):
-        take(len(PARTS) + i, far[i])
-    for copy in kept_copies[len(PARTS) :]:
-        copy.wait()
-
-    for index, dest in enumerate(others):
-        coef = halves(ref["coef"][slot(dest)])
-        for job in across_jobs if index < half else beside_jobs:
-            src, dst = emit(index, dest, job, coef)
-            send(src, dst, ref["back_s"].at[index, job[0]], ref["back_r"].at[me, job[0]], "cols", dest)
-    coef = halves(ref["coef"][slot(me)])
-    local = []
-    for job in beside_jobs:
-        src, dst = emit(len(others), me, job, coef)
-        local.append(pltpu.make_async_copy(src, dst, ref["home"].at[job[0]]))
-        local[-1].start()
-    for index, source in enumerate(others):
-        for i, _, _, start, stop, far_rows in across_jobs if index < half else beside_jobs:
-            dst = place(mirror(source) if far_rows else source, start, stop)
-            remote(
-                dst, dst, ref["back_s"].at[index, i], ref["back_r"].at[source, i], "cols", source
-            ).wait_recv()
-    for copy in local:
-        copy.wait()
-    for copy in sent:
-        copy.wait_send()
+    def place(owner, at):
+        return out_ref.at[owner, pl.ds(at[0], at[1] - at[0])]
+
+    end = at_end(me)
+    inner = jnp.logical_not(end)
+    jobs = [(i, near[i], at, False) for i, at in enumerate(near_at)]
+    jobs += [(len(PARTS) + i, far[i], at, True) for i, at in enumerate(far_at)]
+
+    def when_of(job, crossing, whose):
+        _, _, at, is_far = job
+        if is_far:
+            return False if crossing else at_end(whose)
+        if crossing and at[0] < kept:
+            return jnp.logical_not(at_end(whose))
+        return None
+
+    def emit(n, dest, job):
+        number, buffer, at, is_far = job
+        when = when_of(job, n < half, me)
+        if when is False:
+            return
+        base = slab if is_far else 0
+        src = ref["piece"].at[n, pl.ds(base + at[0], at[1] - at[0])]
+
+        def fill():
+            src[...] = make(dest, halves(ref["coef"][slot(dest)]), buffer)
+
+        if when is None:
+            fill()
+        else:
+            pl.when(when)(fill)
+        dst = place(mirror(me) if is_far else me, at)
+        send(src, dst, ref["back_s"].at[n, number], ref["back_r"].at[me, number], "cols", dest, when=when)
+
+    for job in jobs:
+        i = job[0] - len(PARTS)
+        if i == 0:
+            for k in range(len(EXTRAS)):
+                pl.when(end)(partial(take, len(PARTS) + k, far[k]))
+                pl.when(end)(far_keep[k].wait)
+        for n, dest in enumerate(others):
+            emit(n, dest, job)
+    for number, buffer, at, is_far in jobs:
+
+        def fill(buffer=buffer, at=at, is_far=is_far):
+            place(mirror(me) if is_far else me, at)[...] = make(me, halves(ref["coef"][slot(me)]), buffer)
+
+        if is_far:
+            pl.when(end)(fill)
+        else:
+            fill()
+    for n, source in enumerate(others):
+        for job in jobs:
+            when = when_of(job, n < half, source)
+            if when is False:
+                continue
+            dst = place(mirror(source) if job[3] else source, job[2])
+            copy = remote(dst, dst, ref["back_s"].at[n, job[0]], ref["back_r"].at[source, job[0]], "cols", source)
+            if when is None:
+                copy.wait_recv()
+            else:
+                pl.when(when)(copy.wait_recv)
+    for copy, when in sent:
+        if when is None:
+            copy.wait_send()
+        else:
+            pl.when(when)(copy.wait_send)
+
+
+def band_place(g, i):
+    sizes = [BAND, 2 * BAND, BAND, BAND, 2 * BAND, BAND] + [2 * BAND] * 4
+    return g * sum(sizes) + sum(sizes[:i]), sizes[i]
 
 
 def rotate(groups, band_ref, coef_ref, turn_ref, gram, turn):
@@ -334,8 +377,8 @@
     lo, hi = slice(0, w), slice(w, 2 * w)
 
     def bands(g, i):
-        start = (g * PAIRS + i) * 2 * BAND
-        return band_ref[start : start + 2 * BAND, :]
+        start, size = band_place(g, i)
+        return band_ref[start : start + size, :]
 
     def reset_turns():
         shape = turn.shape
@@ -361,9 +404,16 @@
 
     for g in range(groups):
         for p in range(2):
+            at = 2 * g + p
             below = bands(g, 3 * p + 1)
-            above = to_bands(from_bands(below).T)
-            put_gram(2 * g + p, bands(g, 3 * p), above, below, bands(g, 3 * p + 2))
+            gram[0, BAND:, at, :] = bands(g, 3 * p)
+            gram[1, :, at, :] = to_bands(from_bands(below).T)
+            gram[0, :, pairs + at, :] = below
+            gram[1, BAND:, pairs + at, :] = bands(g, 3 * p + 2)
+    for k, sides in ((0, slice(0, pairs)), (1, slice(pairs, 2 * pairs))):
+        gram[k, 0, sides, :] = jnp.zeros((pairs, w), jnp.float32)
+        for d in range(1, BAND):
+            gram[k, BAND - d, sides, :] = pltpu.roll(gram[k, BAND + d, sides, :], d, 1)
     reset_turns()
     turn_pairs(gram, turn, pairs)
     put_turns(0)
@@ -411,33 +461,35 @@
     groups = count // 4
     f32 = jnp.float32
     block = 8 * split * count
-    total = -(-groups * PAIRS * 2 * BAND // block) * block
+    total = -(-band_place(groups, 0)[0] // block) * block
     piece = total // (split * count)
     extra = sum(EXTRAS) * unit
     segments = len(PARTS) + len(EXTRAS)
-    peers = max(count, split)
     dma = pltpu.SemaphoreType.DMA
     scratch = {
         "acc": pltpu.VMEM((groups, 3, 2 * w, 2 * w), f32),
-        "bands": pltpu.VMEM((split, total // split // (2 * BAND), 2 * BAND, w), f32),
-        "landed": pltpu.VMEM((split, total // split // (2 * BAND), 2 * BAND, w), f32),
+        "bands": pltpu.VMEM((total, w), f32),
+        "landed": pltpu.VMEM((split, count, piece, w), f32),
         "part": pltpu.VMEM((count, piece, w), f32),
         "slots": pltpu.VMEM((count, piece, w), f32),
-        "whole": pltpu.VMEM((count, piece, w), f32),
-        "summed": pltpu.VMEM((split, count, piece, w), f32),
+        "summed": pltpu.VMEM((total, w), f32),
         "turn_of": pltpu.VMEM((groups, 4, 2 * w, 2 * w), f32),
         "gram": pltpu.VMEM((2, 2 * BAND, 4 * groups, w), f32),
         "turn": pltpu.VMEM((2, 2 * BAND, 4 * groups, w), f32),
         "coef": pltpu.VMEM((4 * groups, 4 * w, w), f32),
-        "piece": pltpu.VMEM((count, slab + extra, w), f32),
-        "give": dma((segments, count - 1)),
+        "piece": pltpu.VMEM((count - 1, slab + extra, w), f32),
+        "give": dma((len(PARTS), count - 1)),
+        "give_s": dma((len(EXTRAS), 4)),
         "get": dma((segments, count)),
         "own": dma((segments,)),
-        "sum_s": dma((4, peers)),
-        "sum_r": dma((4, peers)),
+        "rs_s": dma((split, count)),
+        "rs_r": dma((split, count)),
+        "ag_s": dma((split, count)),
+        "ag_r": dma((split, count)),
+        "sum_s": dma((2, count)),
+        "sum_r": dma((2, count)),
         "back_s": dma((count, segments)),
         "back_r": dma((count, segments)),
-        "home": dma((segments,)),
     }
     for i, size in enumerate(PARTS):
         scratch["near%d" % i] = pltpu.VMEM((count, size * unit, w), f32)
@@ -445,12 +497,12 @@
         scratch["far%d" % i] = pltpu.VMEM((count, size * unit, w), f32)
     out = pl.pallas_call(
         partial(fused_kernel, count, split, unit, tuple(scratch)),
-        out_shape=jax.ShapeDtypeStruct((count, slab, w), f32),
+        out_shape=pltpu.VMEM((count, slab, w), f32),
         in_specs=[
             pl.BlockSpec(memory_space=pltpu.SMEM),
             pl.BlockSpec(memory_space=pl.ANY),
         ],
-        out_specs=pl.BlockSpec(memory_space=pl.ANY),
+        out_specs=pl.BlockSpec(memory_space=pltpu.VMEM),
         scratch_shapes=list(scratch.values()),
         compiler_params=pltpu.CompilerParams(collective_id=1, has_side_effects=True),
     )(pairing, anomalies.reshape(count, slab, w))

time: 135 us -> 119 us (0.88); the launches traced: 133 us -> 119 us
  Pallas kernels: 130 us -> 117 us
  local copies, waits for them, and re-layouts: 3.05 us -> 1.32 us
    pallas_call x1, Pallas kernels: 130 us -> 117 us  [on_device(): pl.pallas_call(partial(fused_kernel, count, split, unit, tuple(scratch)),...]
    unnamed x1, local copies, waits for them, and re-layouts: 3.05 us -> 1.32 us
where the time goes in v2:
time: 119 us
  Pallas kernels  117 us (98%)
  local copies, waits for them, and re-layouts  1.32 us (1%)
    pallas_call x1, Pallas kernels, on_device(): pl.pallas_call(partial(fused_kernel, count, split, unit, tuple(scratch)),...  117 us

profile of v2, /device:TPU:0, one launch (start us, length us, event | category | flops | bytes accessed | tf_op | source)
XLA Modules:
  0.0 118.8 jit_solution(8066440504403094859)
XLA Ops:
  0.0 117.5 %shard_map.28 = f32[8,512,128]{2,1,0:T(8,128)S(1)} custom-call(s32[2,8]{1,0:T(2,128)} %pairing.1, f32[8,512,128]{2,1,0:T(8,128)} %bitcast.3), custom_call_target="tpu_custom_call" | custom-call | tf_op jit(solution)/shard_map/pallas_call | solution.py:498
  117.5 1.3 %copy.4 = f32[4096,128]{1,0:T(8,128)} copy(f32[4096,128]{1,0:T(8,128)S(1)} %bitcast.2) | data formatting | bytes 4194304

commit v3 on v2

--- a/solution.py
+++ b/solution.py
@@ -15,7 +15,8 @@
 HIGHEST = lax.Precision.HIGHEST
 UNITS = 8
 PARTS = (3, 3, 1, 1)
-EXTRAS = (3, 2, 3)
+EXTRAS = (1, 1, 6)
+POINTS = (0, 2, 3)
 
 
 def dot(left, right):
@@ -146,7 +147,6 @@
     across = [(1 - side) * half + (pos + j) % half for j in range(half)]
     beside = [side * half + (pos + j) % half for j in range(1, half)]
     others = across + beside
-    ends = [0, 1, count - 2, count - 1]
     masks = (pairing[0, 0], pairing[1, 0], count - 1)
 
     def at_end(d):
@@ -196,10 +196,17 @@
     def give_far(i, crossing):
         rows = pl.ds(far_at[i][0], far_at[i][1] - far_at[i][0])
         n = len(PARTS) + i
-        for k, dest in enumerate(ends):
-            cross = (dest // half) != side
-            when = cross if crossing else jnp.logical_not(cross) & (dest != me)
+        base = (1 - side if crossing else side) * (count - 2)
+        for e in range(2):
+            dest = base + (me + e) % 2
+            k = e if crossing else 2 + e
+            when = None if crossing else dest != me
             send(x_ref.at[mirror(dest), rows], far[i].at[me], ref["give_s"].at[i, k], ref["get"].at[n, me], "cols", dest, when=when)
+
+    def advance(point):
+        for i, when in enumerate(POINTS):
+            if when == point:
+                give_far(i, True)
 
     def take(number, land):
         for source in others:
@@ -215,14 +222,16 @@
         pl.when(at_end(me))(copy.start)
     for i in range(len(PARTS)):
         give_near(i)
-    for i in range(len(EXTRAS)):
-        give_far(i, False)
-    give_far(0, True)
+
+    for e in range(len(EXTRAS)):
+        give_far(e, False)
 
     acc, bands = ref["acc"], ref["bands"]
     for i, land in enumerate(near):
         near_keep[i].wait()
         take(i, land)
+        if i == len(near) - 1:
+            advance(0)
         for g in range(groups):
             x = [land[q] for q in quad_blocks(pairing, count, g)]
             a = jnp.concatenate(x[:2], axis=1)
@@ -246,6 +255,7 @@
         for d in range(1, split):
             peer = (r + d) % split
             send(bands.at[at(peer, c)], landed.at[d, k], ref["rs_s"].at[d, k], ref["rs_r"].at[d, k], "rows", peer)
+    advance(1)
     for k, c in enumerate(others + [me]):
         total = bands[at(r, c)]
         for d in range(1, split):
@@ -255,7 +265,7 @@
         part[k] = total
         if k < len(others):
             send(part.at[k], slots.at[me], ref["sum_s"].at[0, k], ref["sum_r"].at[0, me], "cols", c)
-    give_far(1, True)
+    advance(2)
     for c in others:
         remote(slots.at[c], slots.at[c], ref["sum_s"].at[0, 0], ref["sum_r"].at[0, c], "cols", c).wait_recv()
         total = total + slots[c]
@@ -271,11 +281,12 @@
     for k, c in enumerate(others):
         send(mine, mine, ref["sum_s"].at[1, k], ref["sum_r"].at[1, me], "cols", c)
     spread(me, len(others))
-    give_far(2, True)
+    advance(3)
     for k, c in reversed(list(enumerate(others))):
         block = summed.at[at(r, c)]
         remote(block, block, ref["sum_s"].at[1, k], ref["sum_r"].at[1, c], "cols", c).wait_recv()
         spread(c, k)
+    advance(4)
     for d in range(1, split):
         row = (r + d) % split
         for k, c in enumerate(others + [me]):

time: 119 us -> 111 us (0.933)
  Pallas kernels: 117 us -> 109 us
    pallas_call x1, Pallas kernels: 117 us -> 109 us  [on_device(): pl.pallas_call(partial(fused_kernel, count, split, unit, tuple(scratch)),...]
where the time goes in v3:
time: 111 us; the launch traced here: 110 us
  Pallas kernels  109 us (98%)
  local copies, waits for them, and re-layouts  1.32 us (1%)
    pallas_call x1, Pallas kernels, on_device(): pl.pallas_call(partial(fused_kernel, count, split, unit, tuple(scratch)),...  109 us

profile of v3, /device:TPU:0, one launch (start us, length us, event | category | flops | bytes accessed | tf_op | source)
XLA Modules:
  0.0 110.4 jit_solution(13346584681058783217)
XLA Ops:
  0.0 109.1 %shard_map.28 = f32[8,512,128]{2,1,0:T(8,128)S(1)} custom-call(s32[2,8]{1,0:T(2,128)} %pairing.1, f32[8,512,128]{2,1,0:T(8,128)} %bitcast.3), custom_call_target="tpu_custom_call" | custom-call | tf_op jit(solution)/shard_map/pallas_call | solution.py:509
  109.1 1.3 %copy.4 = f32[4096,128]{1,0:T(8,128)} copy(f32[4096,128]{1,0:T(8,128)S(1)} %bitcast.2) | data formatting | bytes 4194304

commit v4 on v3

--- a/solution.py
+++ b/solution.py
@@ -36,13 +36,6 @@
 def halves(value):
     high = value.astype(jnp.bfloat16)
     return high, (value - high.astype(jnp.float32)).astype(jnp.bfloat16)
-
-
-def dot_3(left, right):
-    a, b = halves(left)
-    c, d = halves(right)
-    product = partial(jnp.dot, preferred_element_type=jnp.float32)
-    return product(a, c) + (product(a, d) + product(b, c))
 
 
 def quad_blocks(pairing, count, g):
@@ -344,10 +337,9 @@
 
     for job in jobs:
         i = job[0] - len(PARTS)
-        if i == 0:
-            for k in range(len(EXTRAS)):
-                pl.when(end)(partial(take, len(PARTS) + k, far[k]))
-                pl.when(end)(far_keep[k].wait)
+        if i >= 0:
+            pl.when(end)(partial(take, job[0], job[1]))
+            pl.when(end)(far_keep[i].wait)
         for n, dest in enumerate(others):
             emit(n, dest, job)
     for number, buffer, at, is_far in jobs:
@@ -407,24 +399,28 @@
                     moved = from_bands(turn[1, :, side, :])
                     turn_ref[g, slot + p, row, hi] = pltpu.roll(moved, SHIFTS, 1)
 
-    def put_gram(at, ll, lr, rl, rr):
+    def put_gram(at, ll, rl, rr):
         gram[0, :, at, :] = ll
-        gram[1, :, at, :] = lr
         gram[0, :, pairs + at, :] = rl
         gram[1, :, pairs + at, :] = rr
+
+    def put_above():
+        gram[1, 0, :pairs, :] = jnp.zeros((pairs, w), jnp.float32)
+        for d in range(1 - BAND, BAND):
+            gram[1, BAND + d, :pairs, :] = pltpu.roll(gram[0, BAND - d, pairs:, :], -d % w, 1)
 
     for g in range(groups):
         for p in range(2):
             at = 2 * g + p
             below = bands(g, 3 * p + 1)
             gram[0, BAND:, at, :] = bands(g, 3 * p)
-            gram[1, :, at, :] = to_bands(from_bands(below).T)
             gram[0, :, pairs + at, :] = below
             gram[1, BAND:, pairs + at, :] = bands(g, 3 * p + 2)
     for k, sides in ((0, slice(0, pairs)), (1, slice(pairs, 2 * pairs))):
         gram[k, 0, sides, :] = jnp.zeros((pairs, w), jnp.float32)
         for d in range(1, BAND):
             gram[k, BAND - d, sides, :] = pltpu.roll(gram[k, BAND + d, sides, :], d, 1)
+    put_above()
     reset_turns()
     turn_pairs(gram, turn, pairs)
     put_turns(0)
@@ -447,8 +443,9 @@
         a_lo, b_lo = gram[0, :, a, :], gram[0, :, b, :]
         a_hi = pltpu.roll(gram[1, :, pairs + a, :], SHIFTS, 1)
         b_hi = pltpu.roll(gram[1, :, pairs + b, :], SHIFTS, 1)
-        put_gram(a, a_lo, to_bands(below[0].T), to_bands(below[0]), b_lo)
-        put_gram(b, a_hi, to_bands(below[1].T), to_bands(below[1]), b_hi)
+        put_gram(a, a_lo, to_bands(below[0]), b_lo)
+        put_gram(b, a_hi, to_bands(below[1]), b_hi)
+    put_above()
     reset_turns()
     turn_pairs(gram, turn, pairs)
     put_turns(2)

time: 111 us -> 111 us (level)
  no operation moved by 1% of the time
where the time goes in v4:
time: 111 us; the launch traced here: 110 us
  Pallas kernels  109 us (98%)
  local copies, waits for them, and re-layouts  1.32 us (1%)
    pallas_call x1, Pallas kernels, on_device(): pl.pallas_call(partial(fused_kernel, count, split, unit, tuple(scratch)),...  109 us

profile of v4, /device:TPU:0, one launch (start us, length us, event | category | flops | bytes accessed | tf_op | source)
XLA Modules:
  0.0 110.4 jit_solution(12795393581319922855)
XLA Ops:
  0.0 109.0 %shard_map.28 = f32[8,512,128]{2,1,0:T(8,128)S(1)} custom-call(s32[2,8]{1,0:T(2,128)} %pairing.1, f32[8,512,128]{2,1,0:T(8,128)} %bitcast.3), custom_call_target="tpu_custom_call" | custom-call | tf_op jit(solution)/shard_map/pallas_call | solution.py:506
  109.0 1.3 %copy.4 = f32[4096,128]{1,0:T(8,128)} copy(f32[4096,128]{1,0:T(8,128)S(1)} %bitcast.2) | data formatting | bytes 4194304
